TPU v7x, 32 devices: a whole 2x2x4 slice. The times are simulated.
32 devices in a mesh: chaos: 4 (over z), gx: 4 (over y, x), gy: 2 (over core).
Axes of the slice: x: 2, y: 2, z: 4, core: 2. Of those that a mesh axis runs over, the one named last changes fastest.
Arguments:
- lam_start: float32 [286, 16, 512], P(None, ('chaos', 'gy'), 'gx'), may hold values from -6 to 6
- adj_source: float32 [286, 16, 512], P(None, ('chaos', 'gy'), 'gx'), may hold values from -6 to 6
- coef_points: float32 [512, 4, 4, 512], P('chaos', None, 'gy', 'gx'), may hold values from 0.1 to 1
- quad_index: int32 [512, 10], replicated, may hold values from 0 to 3
- mode_index: int32 [286, 10], replicated, may hold values from 0 to 3, as said below
Outputs:
- lam_end: float32 [286, 16, 512], P(None, ('chaos', 'gy'), 'gx')
Inputs may be any that keep to these rules, and one draw needn't show every extreme that they name: `mode_index`: each row is a multi-index whose degrees sum to at most 3; each such multi-index of 10 inputs appears exactly once.
All inputs are finite; a program needn't handle non-finite values.
Results may differ from a plain program's by a relative error of at most 0.00011.
Values sent between devices are 32-bit elements; how exact they have to be, the bound alone decides.
A program may use at most 64 MiB of HBM per device.

v0:
```python
import math
import jax
import jax.numpy as jnp
from jax import lax
from jax.sharding import PartitionSpec as P

STEPS = 2
gauss_nodes = (-2.3344142183389773, -0.7419637843027259, 0.7419637843027259, 2.3344142183389773)
gauss_weights = (0.04587585476806849, 0.4541241452319315, 0.4541241452319315, 0.04587585476806849)
mass_shift = 1.0
relax_rate = 0.2
top_prec = lax.Precision.HIGHEST


def tables(quad_index, mode_index):
    node_vals = jnp.array(gauss_nodes, jnp.float32)
    node_wts = jnp.array(gauss_weights, jnp.float32)
    hermite = jnp.stack(
        [
            jnp.ones_like(node_vals),
            node_vals,
            (node_vals * node_vals - 1.0) / math.sqrt(2.0),
            (node_vals * node_vals * node_vals - 3.0 * node_vals) / math.sqrt(6.0),
        ],
        0,
    )
    levels = jnp.arange(4, dtype=jnp.int32)
    quad_hot = (quad_index[:, :, None] == levels[None, None, :]).astype(jnp.float32)
    mode_hot = (mode_index[:, :, None] == levels[None, None, :]).astype(jnp.float32)
    at_nodes = jnp.einsum("qdk,nk->qdn", quad_hot, hermite, precision=top_prec)
    factors = jnp.einsum("qdn,pdn->qpd", at_nodes, mode_hot, precision=top_prec)
    chaos_basis = jnp.prod(factors, axis=2)
    point_wts = jnp.prod(jnp.sum(quad_hot * node_wts[None, None, :], axis=2), axis=1)
    point_wts = point_wts / jnp.sum(point_wts)
    back_map = chaos_basis * point_wts[:, None]
    return (chaos_basis, back_map)


def shift_pair(low, high, axis):
    size = lax.axis_size(axis)
    up = [(i, (i + 1) % size) for i in range(size)]
    down = [(j, i) for i, j in up]
    return (lax.ppermute(high, axis, up), lax.ppermute(low, axis, down))


def local(lam_start, adj_source, coef_points, quad_index, mode_index):
    modes, row_len, col_len = lam_start.shape
    points = quad_index.shape[0]
    rows = ("chaos", "gy")
    row_dev = lax.axis_index(rows)
    row_devs = lax.axis_size(rows)
    keep_low = jnp.where(row_dev == 0, 0.0, 1.0).astype(jnp.float32)
    keep_high = jnp.where(row_dev == row_devs - 1, 0.0, 1.0).astype(jnp.float32)
    coef = lax.all_to_all(coef_points, "chaos", split_axis=1, concat_axis=0, tiled=True)
    coef = coef.reshape(points, row_len, col_len)
    k_low, k_high = shift_pair(coef[:, 0], coef[:, -1], rows)
    k_left, k_right = shift_pair(coef[:, :, :1], coef[:, :, -1:], "gx")
    chaos_basis, back_map = tables(quad_index, mode_index)
    coef_y = [k_low * keep_low] + [coef[:, r] for r in range(row_len)] + [k_high * keep_high]
    coef_x = [jnp.concatenate([k_left[:, r], coef[:, r], k_right[:, r]], 1) for r in range(row_len)]
    lam_now = lam_start
    for repeat in range(STEPS):
        v_low, v_high = shift_pair(lam_now[:, :2], lam_now[:, -2:], rows)
        v_left, v_right = shift_pair(lam_now[:, :, :2], lam_now[:, :, -2:], "gx")
        v_low = v_low * keep_low
        v_high = v_high * keep_high
        parts = (
            [v_low[:, 0], v_low[:, 1]]
            + [lam_now[:, r] for r in range(row_len)]
            + [v_high[:, 0], v_high[:, 1]]
        )
        edges = [v_left[:, r] for r in range(row_len)] + [v_right[:, r] for r in range(row_len)]
        u = jnp.dot(
            chaos_basis,
            jnp.concatenate(parts + edges, 1),
            precision=top_prec,
            preferred_element_type=jnp.float32,
        )
        u_row = [u[:, i * col_len : (i + 1) * col_len] for i in range(row_len + 4)]
        base = (row_len + 4) * col_len
        u_left = [u[:, base + 2 * r : base + 2 * r + 2] for r in range(row_len)]
        base += 2 * row_len
        u_right = [u[:, base + 2 * r : base + 2 * r + 2] for r in range(row_len)]
        flux_y = [coef_y[i] * ((u_row[i + 2] - u_row[i]) * 0.5) for i in range(row_len + 2)]
        div = []
        for r in range(row_len):
            wide = jnp.concatenate([u_left[r], u_row[r + 2], u_right[r]], 1)
            flux_x = coef_x[r] * ((wide[:, 2:] - wide[:, :-2]) * 0.5)
            div.append((flux_x[:, 2:] - flux_x[:, :-2]) * 0.5 + (flux_y[r + 2] - flux_y[r]) * 0.5)
        back = jnp.dot(
            back_map.T,
            jnp.concatenate(div, 1),
            precision=top_prec,
            preferred_element_type=jnp.float32,
        )
        divergence = back.reshape(modes, row_len, col_len)
        lam_now = lam_now + relax_rate * (adj_source - (mass_shift * lam_now - divergence))
    return lam_now


def solution(mesh):
    placed = (
        P(None, ("chaos", "gy"), "gx"),
        P(None, ("chaos", "gy"), "gx"),
        P("chaos", None, "gy", "gx"),
        P(),
        P(),
    )
    return jax.shard_map(
        local, mesh=mesh, in_specs=placed, out_specs=P(None, ("chaos", "gy"), "gx"), check_vma=False
    )
```

profile of v0, /device:TPU:0, one launch (start us, length us, event | category | flops | bytes accessed | tf_op | source)
XLA Modules:
  0.0 80.5 jit_solution(6977557665041020564)
XLA Ops:
  0.0 1.0 %copy.78 = f32[286,2,128]{2,0,1:T(8,128)S(1)} copy(f32[286,2,128]{2,1,0:T(2,128)} %param.7) | data formatting | bytes 585728 | tf_op args[0]
  1.0 4.5 %collective-permute-start.3 = (f32[286,2,128]{2,0,1:T(8,128)S(1)}, f32[286,2,128]{2,0,1:T(8,128)S(1)}, u32[]{:S(2)}, u32[]{:S(2)}) collective-permute-start(f32[286,2,128]{2,0,1:T(8,128)S(1)} %copy.78), channel_id=1, source_target_pairs={{1,0},{8,1},{9,8},{16,9},{17,16},{24,17},{25,24},{0,25},{3,2},{10,... | collective-permute-start | bytes 878600 | tf_op jit(solution)/shard_map/ppermute | solution.py:43
  5.5 2.0 %copy.67 = f32[128,4,2,128]{3,2,0,1:T(2,128)} copy(f32[128,4,2,128]{3,2,1,0:T(2,128)} %param.9) | data formatting | bytes 1048576 | tf_op args[2]
  7.6 3.6 %all-to-all-start = ((f32[128,4,2,128]{3,2,0,1:T(2,128)}), f32[128,4,2,128]{3,2,0,1:T(2,128)S(1)}, u32[]{:S(2)}, u32[]{:S(2)}) async-start(f32[128,4,2,128]{3,2,0,1:T(2,128)} %copy.67), calls=%async_computation | async-start | bytes 1048576 | tf_op jit(solution)/shard_map/all_to_all | solution.py:54
  11.3 2.5 %collective-permute-start.5 = (f32[286,2,2]{2,0,1:T(8,128)S(1)}, f32[286,2,2]{2,0,1:T(8,128)S(1)}, u32[]{:S(2)}, u32[]{:S(2)}) collective-permute-start(f32[286,2,2]{2,0,1:T(8,128)S(1)} %get-tuple-element.35), channel_id=1, source_target_pairs={{2,0},{4,2},{6,4},{0,6},{3,1},{5,3},{7,5},{1,7},{10,8},{12,10},{14... | collective-permute-start | bytes 13736 | tf_op jit(solution)/shard_map/ppermute | solution.py:43
  14.6 1.2 %broadcast_divide_fusion = f32[512]{0:T(512)} fusion(f32[512]{0:T(512)S(1)} %reduce_prod.19, f32[]{:T(128)} %reduce_sum.19), kind=kLoop, calls=%fused_computation.109 | loop fusion | flops 512 | bytes 4100 | tf_op jit(solution)/shard_map/div | solution.py:34
  16.1 3.4 %convolution_reduce_fusion = f32[286,512]{1,0:T(8,128)S(1)} fusion(f32[512,10,4]{0,2,1:T(4,128)S(1)} %fusion.54, s32[286,10]{0,1:T(8,128)} %param.11), kind=kOutput, calls=%fused_computation | convolution fusion | flops 71616688 | bytes 679088 | tf_op jit(solution)/shard_map/qdn,pdn->qpd/dot_general | solution.py:31
  19.5 1.4 %collective-permute-done.5 = f32[286,2,2]{2,0,1:T(8,128)S(1)} collective-permute-done((f32[286,2,2]{2,0,1:T(8,128)S(1)}, f32[286,2,2]{2,0,1:T(8,128)S(1)}, u32[]{:S(2)}, u32[]{:S(2)}) %collective-permute-start.5) | collective-permute-done | bytes 4608 | tf_op jit(solution)/shard_map/ppermute | solution.py:43
  20.9 7.3 %collective-permute-done.4 = f32[286,2,2]{2,0,1:T(8,128)S(1)} collective-permute-done((f32[286,2,2]{2,0,1:T(8,128)S(1)}, f32[286,2,2]{2,0,1:T(8,128)S(1)}, u32[]{:S(2)}, u32[]{:S(2)}) %collective-permute-start.4) | collective-permute-done | bytes 4608 | tf_op jit(solution)/shard_map/ppermute | solution.py:43
  28.3 1.2 %concatenate.47 = f32[286,776]{1,0:T(8,128)} concatenate(f32[286,128]{1,0:T(8,128)S(1)} %get-tuple-element.44, f32[286,128]{1,0:T(8,128)S(1)} %get-tuple-element.43, f32[286,128]{1,0:T(8,128)S(1)} %get-tuple-element.42, f32[286,128]{1,0:T(8,128)S(1)} %get-tuple-element.41, f32[286,128]{1,0:T(8,128)S(1)} %get-tuple-element.40, f32[286,128]{1,0:T(8,128)S(1)} %get-tuple-element.39, ...), dimensions={1} | concatenate | bytes 1775488 | tf_op jit(solution)/shard_map/concatenate | solution.py:75
  29.5 3.9 %fusion.65 = f32[512,776]{0,1:T(8,128)S(1)} fusion(f32[286,512]{1,0:T(8,128)S(1)} %convolution_reduce_fusion, f32[286,776]{1,0:T(8,128)} %concatenate.47), kind=kOutput, calls=%fused_computation.118 | convolution fusion | flops 1363574784 | bytes 3062720 | tf_op jit(solution)/shard_map/dot_general | solution.py:73
  33.5 1.4 %fusion.62 = (f32[512,2,1]{2,1,0:T(2,128)S(1)}, f32[512,2,1]{2,1,0:T(2,128)}) fusion(f32[512,2,128]{2,1,0:T(2,128)S(1)} %bitcast.66), kind=kLoop, calls=%fused_computation.115 | loop fusion | bytes 16384 | tf_op jit(solution)/shard_map/slice | solution.py:57
  34.9 1.2 %copy.97 = f32[512,2,1]{0,2,1:T(1,128)S(1)} copy(f32[512,2,1]{2,1,0:T(2,128)} %get-tuple-element.20) | data formatting | bytes 8192
  36.1 1.5 %collective-permute-start.1 = (f32[512,2,1]{0,2,1:T(1,128)S(1)}, f32[512,2,1]{0,2,1:T(1,128)S(1)}, u32[]{:S(2)}, u32[]{:S(2)}) collective-permute-start(f32[512,2,1]{0,2,1:T(1,128)S(1)} %copy.97), channel_id=1, source_target_pairs={{2,0},{4,2},{6,4},{0,6},{3,1},{5,3},{7,5},{1,7},{10,8},{12,10},{14... | collective-permute-start | bytes 12296 | tf_op jit(solution)/shard_map/ppermute | solution.py:43
  37.6 1.2 %fusion.61 = (f32[512,1,128]{2,1,0:T(1,128)}, f32[512,1,128]{2,1,0:T(1,128)}) fusion(f32[512,2,128]{2,1,0:T(2,128)S(1)} %bitcast.67), kind=kLoop, calls=%fused_computation.114 | loop fusion | bytes 1048576 | tf_op jit(solution)/shard_map/slice | solution.py:60
  38.7 1.1 %copy.96 = f32[512,1,128]{0,2,1:T(8,128)S(1)} copy(f32[512,1,128]{2,1,0:T(1,128)} %get-tuple-element.17) | data formatting | bytes 524288
  39.8 1.1 %copy.98 = f32[512,1,128]{0,2,1:T(8,128)S(1)} copy(f32[512,1,128]{2,1,0:T(1,128)} %get-tuple-element.18) | data formatting | bytes 524288
  41.0 3.5 %collective-permute-start.7 = (f32[512,128]{0,1:T(8,128)S(1)}, f32[512,128]{0,1:T(8,128)}, u32[]{:S(2)}, u32[]{:S(2)}) collective-permute-start(f32[512,128]{0,1:T(8,128)S(1)} %bitcast.68), channel_id=1, source_target_pairs={{1,0},{8,1},{9,8},{16,9},{17,16},{24,17},{25,24},{0,25},{3,2},{10,... | collective-permute-start | bytes 786440 | tf_op jit(solution)/shard_map/ppermute | solution.py:43
  45.3 3.9 %collective-permute-done = f32[512,2,1]{0,2,1:T(1,128)S(1)} collective-permute-done((f32[512,2,1]{0,2,1:T(1,128)S(1)}, f32[512,2,1]{0,2,1:T(1,128)S(1)}, u32[]{:S(2)}, u32[]{:S(2)}) %collective-permute-start) | collective-permute-done | bytes 4128 | tf_op jit(solution)/shard_map/ppermute | solution.py:43
  49.8 1.1 %fusion.51 = (f32[512,128]{0,1:T(8,128)S(1)}, f32[512,128]{0,1:T(8,128)S(1)}) fusion(f32[512,776]{0,1:T(8,128)S(1)} %copy-done.1, f32[512,130]{0,1:T(8,128)S(1)} %fusion.19, f32[512,128]{0,1:T(8,128)} %collective-permute-done.6, f32[]{:T(128)S(6)} %select_n.7, f32[512,1,128]{0,2,1:T(8,128)S(1)} %copy.98), kind=kLoop, calls=%fused_computation.70 | loop fusion | flops 720896 | bytes 2621444 | tf_op jit(solution)/shard_map/add | solution.py:89
  51.1 1.2 %fusion.44 = f32[512,128]{0,1:T(8,128)S(1)} fusion(f32[512,776]{0,1:T(8,128)S(1)} %copy-done.1, f32[512,130]{0,1:T(8,128)S(1)} %fusion.21, f32[512,128]{0,1:T(8,128)} %collective-permute-done.7, f32[]{:T(128)S(6)} %select_n.8, f32[512,1,128]{0,2,1:T(8,128)S(1)} %copy.96), kind=kLoop, calls=%fused_computation.60 | loop fusion | flops 720896 | bytes 2097156 | tf_op jit(solution)/shard_map/add | solution.py:89
  53.5 2.1 %collective-permute-start.9 = (f32[286,2,128]{2,0,1:T(8,128)S(1)}, f32[286,2,128]{2,0,1:T(8,128)S(1)}, u32[]{:S(2)}, u32[]{:S(2)}) collective-permute-start(f32[286,2,128]{2,0,1:T(8,128)S(1)} %fusion.15), channel_id=1, source_target_pairs={{1,0},{8,1},{9,8},{16,9},{17,16},{24,17},{25,24},{0,25},{3,2},{10,... | collective-permute-start | bytes 878600 | tf_op jit(solution)/shard_map/ppermute | solution.py:43
  55.7 1.5 %collective-permute-start.10 = (f32[286,2,2]{2,0,1:T(8,128)S(1)}, f32[286,2,2]{2,0,1:T(8,128)S(1)}, u32[]{:S(2)}, u32[]{:S(2)}) collective-permute-start(f32[286,2,2]{2,0,1:T(8,128)S(1)} %get-tuple-element.24), channel_id=1, source_target_pairs={{0,2},{2,4},{4,6},{6,0},{1,3},{3,5},{5,7},{7,1},{8,10},{10,12},{12... | collective-permute-start | bytes 13736 | tf_op jit(solution)/shard_map/ppermute | solution.py:43
  57.2 6.2 %collective-permute-done.11 = f32[286,2,2]{2,0,1:T(8,128)S(1)} collective-permute-done((f32[286,2,2]{2,0,1:T(8,128)S(1)}, f32[286,2,2]{2,0,1:T(8,128)S(1)}, u32[]{:S(2)}, u32[]{:S(2)}) %collective-permute-start.11) | collective-permute-done | bytes 4608 | tf_op jit(solution)/shard_map/ppermute | solution.py:43
  63.3 6.4 %collective-permute-done.10 = f32[286,2,2]{2,0,1:T(8,128)S(1)} collective-permute-done((f32[286,2,2]{2,0,1:T(8,128)S(1)}, f32[286,2,2]{2,0,1:T(8,128)S(1)}, u32[]{:S(2)}, u32[]{:S(2)}) %collective-permute-start.10) | collective-permute-done | bytes 4608 | tf_op jit(solution)/shard_map/ppermute | solution.py:43
  70.5 0.7 slice_bitcast_fusion.4
  71.2 0.7 slice_bitcast_fusion.8
  71.9 1.4 %concatenate.54 = f32[286,776]{1,0:T(8,128)S(1)} concatenate(f32[286,128]{1,0:T(8,128)} %get-tuple-element.32, f32[286,128]{1,0:T(8,128)} %get-tuple-element.31, f32[286,128]{1,0:T(8,128)S(1)} %get-tuple-element.30, f32[286,128]{1,0:T(8,128)S(1)} %get-tuple-element.29, f32[286,128]{1,0:T(8,128)} %get-tuple-element.28, f32[286,128]{1,0:T(8,128)} %get-tuple-element.27, ...), dimensions={1} | concatenate | bytes 1775488 | tf_op jit(solution)/shard_map/concatenate | solution.py:75
  73.3 2.7 %fusion.66 = f32[512,776]{0,1:T(8,128)S(1)} fusion(f32[286,512]{1,0:T(8,128)S(1)} %convolution_reduce_fusion, f32[286,776]{1,0:T(8,128)S(1)} %concatenate.54), kind=kOutput, calls=%fused_computation.119 | convolution fusion | flops 1363574784 | bytes 3062720 | tf_op jit(solution)/shard_map/dot_general | solution.py:73
  76.2 1.1 %fusion.37 = (f32[512,128]{0,1:T(8,128)S(1)}, f32[512,128]{0,1:T(8,128)S(1)}) fusion(f32[512,776]{0,1:T(8,128)S(1)} %fusion.66, f32[512,130]{0,1:T(8,128)S(1)} %fusion.23, f32[512,128]{0,1:T(8,128)} %collective-permute-done.6, f32[]{:T(128)S(6)} %select_n.7, f32[512,1,128]{0,2,1:T(8,128)S(1)} %copy.98), kind=kLoop, calls=%fused_computation.50 | loop fusion | flops 720896 | bytes 2621444 | tf_op jit(solution)/shard_map/add | solution.py:89
  77.5 1.1 %fusion.30 = f32[512,128]{0,1:T(8,128)S(1)} fusion(f32[512,776]{0,1:T(8,128)S(1)} %fusion.66, f32[512,130]{0,1:T(8,128)S(1)} %fusion.25, f32[512,128]{0,1:T(8,128)} %collective-permute-done.7, f32[]{:T(128)S(6)} %select_n.8, f32[512,1,128]{0,2,1:T(8,128)S(1)} %copy.96), kind=kLoop, calls=%fused_computation.40 | loop fusion | flops 720896 | bytes 2097156 | tf_op jit(solution)/shard_map/add | solution.py:89
  79.5 0.9 %copy.89 = f32[286,2,128]{2,1,0:T(2,128)} copy(f32[286,2,128]{2,0,1:T(8,128)S(1)} %fusion.12) | data formatting | bytes 585728 | tf_op jit(solution)/shard_map/add | solution.py:97
  (84 shorter events, 5.8 us)
Async XLA Ops:
  1.0 27.2 %collective-permute-start.3 = (f32[286,2,128]{2,0,1:T(8,128)S(1)}, f32[286,2,128]{2,0,1:T(8,128)S(1)}, u32[]{:S(2)}, u32[]{:S(2)}) collective-permute-start(f32[286,2,128]{2,0,1:T(8,128)S(1)} %copy.78), channel_id=1, source_target_pairs={{1,0},{8,1},{9,8},{16,9},{17,16},{24,17},{25,24},{0,25},{3,2},{10,... | collective-permute-start | bytes 878600 | tf_op jit(solution)/shard_map/ppermute | solution.py:43
  5.5 22.7 %collective-permute-start.2 = (f32[286,2,128]{2,0,1:T(8,128)S(1)}, f32[286,2,128]{2,0,1:T(8,128)S(1)}, u32[]{:S(2)}, u32[]{:S(2)}) collective-permute-start(f32[286,2,128]{2,0,1:T(8,128)S(1)} %copy.78), channel_id=1, source_target_pairs={{0,1},{1,8},{8,9},{9,16},{16,17},{17,24},{24,25},{25,0},{2,3},{3,1... | collective-permute-start | bytes 878600 | tf_op jit(solution)/shard_map/ppermute | solution.py:43
  7.6 6.3 %copy-start.4 = (s32[512,10]{0,1:T(8,128)S(1)}, s32[512,10]{0,1:T(8,128)}, u32[]{:S(2)}) copy-start(s32[512,10]{0,1:T(8,128)} %param.10) | copy-start | bytes 61444
  7.6 6.3 %copy-start.16 = (f32[4]{0:T(128)S(1)}, f32[4]{0:T(128)}, u32[]{:S(2)}) copy-start(f32[4]{0:T(128)} %constant.42.clone) | copy-start | bytes 52
  7.6 8.3 %copy-start.15 = (f32[4,4,1]{1,0,2:T(4,128)S(1)}, f32[4,4,1]{1,0,2:T(4,128)}, u32[]{:S(2)}) copy-start(f32[4,4,1]{1,0,2:T(4,128)} %constant.56) | copy-start | bytes 196
  7.6 25.9 %all-to-all-start = ((f32[128,4,2,128]{3,2,0,1:T(2,128)}), f32[128,4,2,128]{3,2,0,1:T(2,128)S(1)}, u32[]{:S(2)}, u32[]{:S(2)}) async-start(f32[128,4,2,128]{3,2,0,1:T(2,128)} %copy.67), calls=%async_computation | async-start | bytes 1048576 | tf_op jit(solution)/shard_map/all_to_all | solution.py:54
  11.3 9.5 %collective-permute-start.5 = (f32[286,2,2]{2,0,1:T(8,128)S(1)}, f32[286,2,2]{2,0,1:T(8,128)S(1)}, u32[]{:S(2)}, u32[]{:S(2)}) collective-permute-start(f32[286,2,2]{2,0,1:T(8,128)S(1)} %get-tuple-element.35), channel_id=1, source_target_pairs={{2,0},{4,2},{6,4},{0,6},{3,1},{5,3},{7,5},{1,7},{10,8},{12,10},{14... | collective-permute-start | bytes 13736 | tf_op jit(solution)/shard_map/ppermute | solution.py:43
  13.8 14.3 %collective-permute-start.4 = (f32[286,2,2]{2,0,1:T(8,128)S(1)}, f32[286,2,2]{2,0,1:T(8,128)S(1)}, u32[]{:S(2)}, u32[]{:S(2)}) collective-permute-start(f32[286,2,2]{2,0,1:T(8,128)S(1)} %get-tuple-element.36), channel_id=1, source_target_pairs={{0,2},{2,4},{4,6},{6,0},{1,3},{3,5},{5,7},{7,1},{8,10},{10,12},{12... | collective-permute-start | bytes 13736 | tf_op jit(solution)/shard_map/ppermute | solution.py:43
  33.5 2.6 %copy-start = (f32[512,776]{0,1:T(8,128)}, f32[512,776]{0,1:T(8,128)S(1)}, u32[]{:S(2)}) copy-start(f32[512,776]{0,1:T(8,128)S(1)} %fusion.65) | copy-start | bytes 4767748
  36.1 9.2 %collective-permute-start.1 = (f32[512,2,1]{0,2,1:T(1,128)S(1)}, f32[512,2,1]{0,2,1:T(1,128)S(1)}, u32[]{:S(2)}, u32[]{:S(2)}) collective-permute-start(f32[512,2,1]{0,2,1:T(1,128)S(1)} %copy.97), channel_id=1, source_target_pairs={{2,0},{4,2},{6,4},{0,6},{3,1},{5,3},{7,5},{1,7},{10,8},{12,10},{14... | collective-permute-start | bytes 12296 | tf_op jit(solution)/shard_map/ppermute | solution.py:43
  37.6 11.7 %slice-start = ((f32[512,776]{0,1:T(8,128)}), f32[512,128]{0,1:T(8,128)S(1)}, s32[]{:S(2)}) async-start(f32[512,776]{0,1:T(8,128)} %copy-done), calls=%async_computation.1 | async-start | bytes 524288 | tf_op jit(solution)/shard_map/slice | solution.py:79
  37.6 12.3 %copy-start.1 = (f32[512,776]{0,1:T(8,128)S(1)}, f32[512,776]{0,1:T(8,128)}, u32[]{:S(2)}) copy-start(f32[512,776]{0,1:T(8,128)} %copy-done) | copy-start | bytes 4767748
  40.9 8.9 %collective-permute-start.6 = (f32[512,128]{0,1:T(8,128)S(1)}, f32[512,128]{0,1:T(8,128)}, u32[]{:S(2)}, u32[]{:S(2)}) collective-permute-start(f32[512,128]{0,1:T(8,128)S(1)} %bitcast.71), channel_id=1, source_target_pairs={{0,1},{1,8},{8,9},{9,16},{16,17},{17,24},{24,25},{25,0},{2,3},{3,1... | collective-permute-start | bytes 786440 | tf_op jit(solution)/shard_map/ppermute | solution.py:43
  41.0 10.1 %collective-permute-start.7 = (f32[512,128]{0,1:T(8,128)S(1)}, f32[512,128]{0,1:T(8,128)}, u32[]{:S(2)}, u32[]{:S(2)}) collective-permute-start(f32[512,128]{0,1:T(8,128)S(1)} %bitcast.68), channel_id=1, source_target_pairs={{1,0},{8,1},{9,8},{16,9},{17,16},{24,17},{25,24},{0,25},{3,2},{10,... | collective-permute-start | bytes 786440 | tf_op jit(solution)/shard_map/ppermute | solution.py:43
  44.7 4.5 %collective-permute-start = (f32[512,2,1]{0,2,1:T(1,128)S(1)}, f32[512,2,1]{0,2,1:T(1,128)S(1)}, u32[]{:S(2)}, u32[]{:S(2)}) collective-permute-start(f32[512,2,1]{0,2,1:T(1,128)S(1)} %copy.95), channel_id=1, source_target_pairs={{0,2},{2,4},{4,6},{6,0},{1,3},{3,5},{5,7},{7,1},{8,10},{10,12},{12... | collective-permute-start | bytes 12296 | tf_op jit(solution)/shard_map/ppermute | solution.py:43
  45.3 4.0 %copy-start.11 = (f32[512,1]{0,1:T(1,128)}, f32[512,1]{0,1:T(1,128)S(1)}, u32[]{:S(2)}) copy-start(f32[512,1]{0,1:T(1,128)S(1)} %get-tuple-element.47) | copy-start | bytes 6148
  45.3 5.7 %copy-start.7 = (f32[512,1]{0,1:T(1,128)}, f32[512,1]{0,1:T(1,128)S(1)}, u32[]{:S(2)}) copy-start(f32[512,1]{0,1:T(1,128)S(1)} %get-tuple-element.48) | copy-start | bytes 6148
  49.2 0.6 copy-start.13
  49.2 1.8 %copy-start.9 = (f32[512,1]{0,1:T(1,128)}, f32[512,1]{0,1:T(1,128)S(1)}, u32[]{:S(2)}) copy-start(f32[512,1]{0,1:T(1,128)S(1)} %get-tuple-element.46) | copy-start | bytes 6148
  51.0 1.3 %copy-start.5 = (f32[512]{0:T(512)S(1)}, f32[512]{0:T(512)}, u32[]{:S(2)}) copy-start(f32[512]{0:T(512)} %broadcast_divide_fusion) | copy-start | bytes 6148
  51.1 2.1 %copy-start.2 = (f32[286,2,128]{2,1,0:T(2,128)S(1)}, f32[286,2,128]{2,1,0:T(2,128)}, u32[]{:S(2)}) copy-start(f32[286,2,128]{2,1,0:T(2,128)} %param.7) | copy-start | bytes 878596
  51.1 2.1 %copy-start.3 = (f32[286,2,128]{2,1,0:T(2,128)S(1)}, f32[286,2,128]{2,1,0:T(2,128)}, u32[]{:S(2)}) copy-start(f32[286,2,128]{2,1,0:T(2,128)} %param.8) | copy-start | bytes 878596
  53.4 9.9 %collective-permute-start.11 = (f32[286,2,2]{2,0,1:T(8,128)S(1)}, f32[286,2,2]{2,0,1:T(8,128)S(1)}, u32[]{:S(2)}, u32[]{:S(2)}) collective-permute-start(f32[286,2,2]{2,0,1:T(8,128)S(1)} %get-tuple-element.23), channel_id=1, source_target_pairs={{2,0},{4,2},{6,4},{0,6},{3,1},{5,3},{7,5},{1,7},{10,8},{12,10},{14... | collective-permute-start | bytes 13736 | tf_op jit(solution)/shard_map/ppermute | solution.py:43
  53.5 16.9 %collective-permute-start.9 = (f32[286,2,128]{2,0,1:T(8,128)S(1)}, f32[286,2,128]{2,0,1:T(8,128)S(1)}, u32[]{:S(2)}, u32[]{:S(2)}) collective-permute-start(f32[286,2,128]{2,0,1:T(8,128)S(1)} %fusion.15), channel_id=1, source_target_pairs={{1,0},{8,1},{9,8},{16,9},{17,16},{24,17},{25,24},{0,25},{3,2},{10,... | collective-permute-start | bytes 878600 | tf_op jit(solution)/shard_map/ppermute | solution.py:43
  55.7 15.5 %collective-permute-start.8 = (f32[286,2,128]{2,0,1:T(8,128)S(1)}, f32[286,2,128]{2,0,1:T(8,128)S(1)}, u32[]{:S(2)}, u32[]{:S(2)}) collective-permute-start(f32[286,2,128]{2,0,1:T(8,128)S(1)} %fusion.15), channel_id=1, source_target_pairs={{0,1},{1,8},{8,9},{9,16},{16,17},{17,24},{24,25},{25,0},{2,3},{3,1... | collective-permute-start | bytes 878600 | tf_op jit(solution)/shard_map/ppermute | solution.py:43
  55.7 14.1 %collective-permute-start.10 = (f32[286,2,2]{2,0,1:T(8,128)S(1)}, f32[286,2,2]{2,0,1:T(8,128)S(1)}, u32[]{:S(2)}, u32[]{:S(2)}) collective-permute-start(f32[286,2,2]{2,0,1:T(8,128)S(1)} %get-tuple-element.24), channel_id=1, source_target_pairs={{0,2},{2,4},{4,6},{6,0},{1,3},{3,5},{5,7},{7,1},{8,10},{10,12},{12... | collective-permute-start | bytes 13736 | tf_op jit(solution)/shard_map/ppermute | solution.py:43
  73.3 2.8 %copy-start.12 = (f32[512,1]{0,1:T(1,128)S(1)}, f32[512,1]{0,1:T(1,128)}, u32[]{:S(2)}) copy-start(f32[512,1]{0,1:T(1,128)} %copy-done.11) | copy-start | bytes 6148
  73.3 2.8 %copy-start.14 = (f32[512,1]{0,1:T(1,128)S(1)}, f32[512,1]{0,1:T(1,128)}, u32[]{:S(2)}) copy-start(f32[512,1]{0,1:T(1,128)} %copy-done.13) | copy-start | bytes 6148
  76.1 1.3 %copy-start.8 = (f32[512,1]{0,1:T(1,128)S(1)}, f32[512,1]{0,1:T(1,128)}, u32[]{:S(2)}) copy-start(f32[512,1]{0,1:T(1,128)} %copy-done.7) | copy-start | bytes 6148
  76.1 1.3 %copy-start.10 = (f32[512,1]{0,1:T(1,128)S(1)}, f32[512,1]{0,1:T(1,128)}, u32[]{:S(2)}) copy-start(f32[512,1]{0,1:T(1,128)} %copy-done.9) | copy-start | bytes 6148
  77.4 1.2 %copy-start.6 = (f32[512]{0:T(512)S(1)}, f32[512]{0:T(512)}, u32[]{:S(2)}) copy-start(f32[512]{0:T(512)} %broadcast_divide_fusion) | copy-start | bytes 6148
where the time goes:
time: 81.1 us; the launch traced here: 80.5 us
  waiting for transfers between devices  25.1 us (31%)
  starting transfers between devices  20 us (25%)
  local copies, waits for them, and re-layouts  16.1 us (20%)
  matrix products  11.6 us (14%)
  other arithmetic  7.13 us (9%)
    ppermute x12, waiting for transfers between devices, shift_pair(): return (lax.ppermute(high, axis, up), lax.ppermute(low, axis, down))  25.1 us
    ppermute x12, starting transfers between devices, shift_pair(): return (lax.ppermute(high, axis, up), lax.ppermute(low, axis, down))  16.4 us
    unnamed x40, local copies, waits for them, and re-layouts  7.13 us
    dot_general x2, matrix products, local(): jnp.dot(chaos_basis, jnp.concatenate(parts + edges, 1), precision=top_pre...  6.67 us
    add x4, other arithmetic, local(): (flux_x[:, 2:] - flux_x[:, :-2]) * 0.5 + (flux_y[r + 2] - flux_y[r]) * 0.5  4.61 us
    all_to_all x1, starting transfers between devices, local(): lax.all_to_all(coef_points, 'chaos', split_axis=1, concat_axis=0, tiled=T...  3.6 us
    dot_general x1, matrix products, tables(): factors = jnp.einsum('qdn,pdn->qpd', at_nodes, mode_hot, precision=top_prec)  3.4 us
    concatenate x2, local copies, waits for them, and re-layouts, local(): jnp.concatenate(parts + edges, 1)  2.57 us
  transfers between devices with their start and end apart: 13, of which 5 were waited for; matrix products, arithmetic and copies ran while one was open for 24% of the time, Pallas kernels for 0%

commit v1 on v0

--- a/solution.py
+++ b/solution.py
@@ -1,8 +1,10 @@
+import functools
 import math
 import jax
 import jax.numpy as jnp
 from jax import lax
 from jax.sharding import PartitionSpec as P
+from jax.lax import axis_index, axis_size, ppermute
 
 STEPS = 2
 gauss_nodes = (-2.3344142183389773, -0.7419637843027259, 0.7419637843027259, 2.3344142183389773)
@@ -10,6 +12,38 @@
 mass_shift = 1.0
 relax_rate = 0.2
 top_prec = lax.Precision.HIGHEST
+
+
+def close_numbers(piece_in, which_dim, chunk):
+    part_next = piece_in.shape
+    mid_arr = piece_in.reshape(
+        *part_next[:which_dim], chunk, part_next[which_dim] // chunk, *part_next[which_dim + 1 :]
+    )
+    return jnp.moveaxis(mid_arr, which_dim, 0)
+
+
+def work_widths_in(s0, d0):
+    s0 = jnp.moveaxis(s0, 0, d0)
+    kept_arr = s0.shape
+    return s0.reshape(*kept_arr[:d0], kept_arr[d0] * kept_arr[d0 + 1], *kept_arr[d0 + 2 :])
+
+
+def set_record(xin, axis_tag, packet, matrix):
+    local_part = axis_size(axis_tag)
+    oldest = axis_index(axis_tag)
+    side_arr, built = (local_part, oldest)
+    reply = close_numbers(xin, packet, side_arr)
+    y1 = reply
+    for src_i in range(1, side_arr):
+        main, ready = ((built + src_i) % side_arr, (built - src_i) % side_arr)
+        x_now = lax.dynamic_index_in_dim(reply, main, 0)
+        prior = map(lambda dev_i: (dev_i, (dev_i + src_i) % side_arr), range(side_arr))
+        s_next = ppermute(x_now, axis_tag, list(prior))
+        y1 = lax.dynamic_update_slice_in_dim(y1, s_next, ready, axis=0)
+    return work_widths_in(y1, matrix)
+
+
+fill_the_modes = functools.partial(set_record, axis_tag="chaos", packet=1, matrix=0)
 
 
 def tables(quad_index, mode_index):
@@ -51,7 +85,7 @@
     row_devs = lax.axis_size(rows)
     keep_low = jnp.where(row_dev == 0, 0.0, 1.0).astype(jnp.float32)
     keep_high = jnp.where(row_dev == row_devs - 1, 0.0, 1.0).astype(jnp.float32)
-    coef = lax.all_to_all(coef_points, "chaos", split_axis=1, concat_axis=0, tiled=True)
+    coef = fill_the_modes(coef_points)
     coef = coef.reshape(points, row_len, col_len)
     k_low, k_high = shift_pair(coef[:, 0], coef[:, -1], rows)
     k_left, k_right = shift_pair(coef[:, :, :1], coef[:, :, -1:], "gx")

time: 81.1 us -> 78.3 us (0.965)
  other arithmetic: 7.13 us -> 4.62 us
  waiting for transfers between devices: 25.1 us -> 27.4 us
  matrix products: 11.6 us -> 9.62 us
    ppermute x0 -> x3, waiting for transfers between devices: none -> 7.84 us  [set_record(): s_next = ppermute(x_now, axis_tag, list(prior))]
    ppermute x12, waiting for transfers between devices: 25.1 us -> 19.6 us  [shift_pair(): return (lax.ppermute(high, axis, up), lax.ppermute(low, axis, down))]
    unnamed x40 -> x18, local copies, waits for them, and re-layouts: 7.13 us -> 3.28 us
    add x4 -> x2, other arithmetic: 4.61 us -> 0.77 us  [local(): (flux_x[:, 2:] - flux_x[:, :-2]) * 0.5 + (flux_y[r + 2] - flux_y[r]) * 0.5]
    all_to_all x1 -> x0, starting transfers between devices: 3.6 us -> none  [local(): lax.all_to_all(coef_points, 'chaos', split_axis=1, concat_axis=0, tiled=T...]
    ppermute x0 -> x3, starting transfers between devices: none -> 2.08 us  [set_record(): s_next = ppermute(x_now, axis_tag, list(prior))]
    ppermute x12, starting transfers between devices: 16.4 us -> 18.3 us  [shift_pair(): return (lax.ppermute(high, axis, up), lax.ppermute(low, axis, down))]
    squeeze x2, local copies, waits for them, and re-layouts: 0.04 us -> 1.47 us  [local(): v_right[:, r]]
  transfers between devices with their start and end apart: 13 -> 15, of which waited for: 5 -> 7; matrix products, arithmetic and copies ran while one was open for 24% -> 22% of each run, Pallas kernels for 0% -> 0%
where the time goes in v1:
time: 78.3 us; the launch traced here: 77.9 us
  waiting for transfers between devices  27.4 us (35%)
  starting transfers between devices  20.4 us (26%)
  local copies, waits for them, and re-layouts  15.4 us (20%)
  matrix products  9.62 us (12%)
  other arithmetic  4.62 us (6%)
    ppermute x12, waiting for transfers between devices, shift_pair(): return (lax.ppermute(high, axis, up), lax.ppermute(low, axis, down))  19.6 us
    ppermute x12, starting transfers between devices, shift_pair(): return (lax.ppermute(high, axis, up), lax.ppermute(low, axis, down))  18.3 us
    ppermute x3, waiting for transfers between devices, set_record(): s_next = ppermute(x_now, axis_tag, list(prior))  7.84 us
    dot_general x2, matrix products, local(): jnp.dot(chaos_basis, jnp.concatenate(parts + edges, 1), precision=top_pre...  5.45 us
    unnamed x18, local copies, waits for them, and re-layouts  3.28 us
    concatenate x2, local copies, waits for them, and re-layouts, local(): jnp.concatenate(parts + edges, 1)  3.07 us
    dot_general x1, matrix products, tables(): factors = jnp.einsum('qdn,pdn->qpd', at_nodes, mode_hot, precision=top_prec)  2.62 us
    ppermute x3, starting transfers between devices, set_record(): s_next = ppermute(x_now, axis_tag, list(prior))  2.08 us
  transfers between devices with their start and end apart: 15, of which 7 were waited for; matrix products, arithmetic and copies ran while one was open for 22% of the time, Pallas kernels for 0%

profile of v1, /device:TPU:0, one launch (start us, length us, event | category | flops | bytes accessed | tf_op | source)
XLA Modules:
  0.0 77.9 jit_solution(11885158355449301248)
XLA Ops:
  0.0 1.0 %copy.91 = f32[128,4,2,128]{3,2,1,0:T(2,128)S(1)} copy(f32[128,4,2,128]{3,2,1,0:T(2,128)} %param.9) | data formatting | bytes 1048576
  1.0 1.0 %copy.54 = f32[286,2,128]{2,0,1:T(8,128)S(1)} copy(f32[286,2,128]{2,1,0:T(2,128)} %param.7) | data formatting | bytes 585728 | tf_op args[0]
  2.1 4.5 %collective-permute-start.6 = (f32[286,2,128]{2,0,1:T(8,128)S(1)}, f32[286,2,128]{2,0,1:T(8,128)}, u32[]{:S(2)}, u32[]{:S(2)}) collective-permute-start(f32[286,2,128]{2,0,1:T(8,128)S(1)} %copy.54), channel_id=1, source_target_pairs={{1,0},{8,1},{9,8},{16,9},{17,16},{24,17},{25,24},{0,25},{3,2},{10,... | collective-permute-start | bytes 878600 | tf_op jit(solution)/shard_map/ppermute | solution.py:77
  6.7 1.1 %collective-permute-start.2 = (f32[1,128,1,2,128]{4,3,0,1,2:T(2,128)S(1)}, f32[1,128,1,2,128]{4,3,0,1,2:T(2,128)S(1)}, u32[]{:S(2)}, u32[]{:S(2)}) collective-permute-start(f32[1,128,1,2,128]{4,3,0,1,2:T(2,128)S(1)} %get-tuple-element.25), channel_id=1, source_target_pairs={{0,24},{8,0},{16,8},{24,16},{1,25},{9,1},{17,9},{25,17},{2,26},{10... | collective-permute-start | bytes 393224 | tf_op jit(solution)/shard_map/ppermute | solution.py:41
  7.9 1.0 %collective-permute-start = (f32[1,128,1,2,128]{4,3,0,1,2:T(2,128)S(1)}, f32[1,128,1,2,128]{4,3,0,1,2:T(2,128)S(1)}, u32[]{:S(2)}, u32[]{:S(2)}) collective-permute-start(f32[1,128,1,2,128]{4,3,0,1,2:T(2,128)S(1)} %get-tuple-element.26), channel_id=1, source_target_pairs={{0,8},{8,16},{16,24},{24,0},{1,9},{9,17},{17,25},{25,1},{2,10},{10... | collective-permute-start | bytes 393224 | tf_op jit(solution)/shard_map/ppermute | solution.py:41
  9.0 2.5 %collective-permute-start.8 = (f32[286,2,2]{2,0,1:T(8,128)S(1)}, f32[286,2,2]{2,0,1:T(8,128)S(1)}, u32[]{:S(2)}, u32[]{:S(2)}) collective-permute-start(f32[286,2,2]{2,0,1:T(8,128)S(1)} %get-tuple-element.42), channel_id=1, source_target_pairs={{2,0},{4,2},{6,4},{0,6},{3,1},{5,3},{7,5},{1,7},{10,8},{12,10},{14... | collective-permute-start | bytes 13736 | tf_op jit(solution)/shard_map/ppermute | solution.py:77
  13.1 2.6 %convolution_reduce_fusion = f32[286,512]{1,0:T(8,128)S(1)} fusion(f32[512,10,4]{0,2,1:T(4,128)S(1)} %fusion.54, s32[286,10]{0,1:T(8,128)S(1)} %copy-done.7), kind=kOutput, calls=%fused_computation | convolution fusion | flops 71616688 | bytes 679088 | tf_op jit(solution)/shard_map/qdn,pdn->qpd/dot_general | solution.py:65
  15.9 2.4 %collective-permute-done.8 = f32[286,2,2]{2,0,1:T(8,128)S(1)} collective-permute-done((f32[286,2,2]{2,0,1:T(8,128)S(1)}, f32[286,2,2]{2,0,1:T(8,128)S(1)}, u32[]{:S(2)}, u32[]{:S(2)}) %collective-permute-start.8) | collective-permute-done | bytes 4608 | tf_op jit(solution)/shard_map/ppermute | solution.py:77
  18.3 2.4 %collective-permute-start.7 = (f32[286,2,2]{2,0,1:T(8,128)S(1)}, f32[286,2,2]{2,0,1:T(8,128)S(1)}, u32[]{:S(2)}, u32[]{:S(2)}) collective-permute-start(f32[286,2,2]{2,0,1:T(8,128)S(1)} %get-tuple-element.43), channel_id=1, source_target_pairs={{0,2},{2,4},{4,6},{6,0},{1,3},{3,5},{5,7},{7,1},{8,10},{10,12},{12... | collective-permute-start | bytes 13736 | tf_op jit(solution)/shard_map/ppermute | solution.py:77
  20.7 0.7 slice_bitcast_fusion.12
  21.4 7.8 %collective-permute-done.7 = f32[286,2,2]{2,0,1:T(8,128)S(1)} collective-permute-done((f32[286,2,2]{2,0,1:T(8,128)S(1)}, f32[286,2,2]{2,0,1:T(8,128)S(1)}, u32[]{:S(2)}, u32[]{:S(2)}) %collective-permute-start.7) | collective-permute-done | bytes 4608 | tf_op jit(solution)/shard_map/ppermute | solution.py:77
  29.2 0.7 slice_bitcast_fusion.14
  30.0 7.8 %collective-permute-done.1 = f32[1,128,1,2,128]{4,3,0,1,2:T(2,128)S(1)} collective-permute-done((f32[1,128,1,2,128]{4,3,0,1,2:T(2,128)S(1)}, f32[1,128,1,2,128]{4,3,0,1,2:T(2,128)S(1)}, u32[]{:S(2)}, u32[]{:S(2)}) %collective-permute-start.1) | collective-permute-done | bytes 131104 | tf_op jit(solution)/shard_map/ppermute | solution.py:41
  38.5 1.0 %collective-permute-start.3 = (f32[512,2,1]{0,2,1:T(1,128)S(1)}, f32[512,2,1]{0,2,1:T(1,128)S(1)}, u32[]{:S(2)}, u32[]{:S(2)}) collective-permute-start(f32[512,2,1]{0,2,1:T(1,128)S(1)} %get-tuple-element.23), channel_id=1, source_target_pairs={{0,2},{2,4},{4,6},{6,0},{1,3},{3,5},{5,7},{7,1},{8,10},{10,12},{12... | collective-permute-start | bytes 12296 | tf_op jit(solution)/shard_map/ppermute | solution.py:77
  39.5 2.1 %collective-permute-start.4 = (f32[512,2,1]{0,2,1:T(1,128)S(1)}, f32[512,2,1]{0,2,1:T(1,128)S(1)}, u32[]{:S(2)}, u32[]{:S(2)}) collective-permute-start(f32[512,2,1]{0,2,1:T(1,128)S(1)} %get-tuple-element.24), channel_id=1, source_target_pairs={{2,0},{4,2},{6,4},{0,6},{3,1},{5,3},{7,5},{1,7},{10,8},{12,10},{14... | collective-permute-start | bytes 12296 | tf_op jit(solution)/shard_map/ppermute | solution.py:77
  42.2 0.9 %collective-permute-done.3 = f32[512,2,1]{0,2,1:T(1,128)S(1)} collective-permute-done((f32[512,2,1]{0,2,1:T(1,128)S(1)}, f32[512,2,1]{0,2,1:T(1,128)S(1)}, u32[]{:S(2)}, u32[]{:S(2)}) %collective-permute-start.3) | collective-permute-done | bytes 4128 | tf_op jit(solution)/shard_map/ppermute | solution.py:77
  43.2 1.0 %broadcast_multiply_fusion.1 = f32[286,2,128]{2,0,1:T(8,128)S(1)} fusion(f32[286,2,128]{2,0,1:T(8,128)} %collective-permute-done.6, f32[]{:T(128)S(6)} %select_n.66), kind=kLoop, calls=%fused_computation.98 | loop fusion | flops 73216 | bytes 585732 | tf_op jit(solution)/shard_map/mul | solution.py:100
  44.9 1.0 %broadcast_multiply_fusion.3 = f32[286,2,128]{2,0,1:T(8,128)S(1)} fusion(f32[286,2,128]{2,0,1:T(8,128)} %collective-permute-done.5, f32[]{:T(128)S(6)} %select_n.65), kind=kLoop, calls=%fused_computation.100 | loop fusion | flops 73216 | bytes 585732 | tf_op jit(solution)/shard_map/mul | solution.py:99
  46.6 1.5 %concatenate.47 = f32[286,776]{1,0:T(8,128)S(1)} concatenate(f32[286,128]{1,0:T(8,128)} %get-tuple-element.51, f32[286,128]{1,0:T(8,128)} %get-tuple-element.50, f32[286,128]{1,0:T(8,128)S(1)} %get-tuple-element.49, f32[286,128]{1,0:T(8,128)S(1)} %get-tuple-element.48, f32[286,128]{1,0:T(8,128)} %get-tuple-element.47, f32[286,128]{1,0:T(8,128)} %get-tuple-element.46, ...), dimensions={1} | concatenate | bytes 1775488 | tf_op jit(solution)/shard_map/concatenate | solution.py:109
  48.1 2.7 %fusion.66 = f32[512,776]{0,1:T(8,128)S(1)} fusion(f32[286,512]{1,0:T(8,128)S(1)} %convolution_reduce_fusion, f32[286,776]{1,0:T(8,128)S(1)} %concatenate.47), kind=kOutput, calls=%fused_computation.127 | convolution fusion | flops 1363574784 | bytes 3062720 | tf_op jit(solution)/shard_map/dot_general | solution.py:107
  53.1 3.0 %collective-permute-start.14 = (f32[286,2,2]{2,0,1:T(8,128)S(1)}, f32[286,2,2]{2,0,1:T(8,128)S(1)}, u32[]{:S(2)}, u32[]{:S(2)}) collective-permute-start(f32[286,2,2]{2,0,1:T(8,128)S(1)} %get-tuple-element.30), channel_id=1, source_target_pairs={{2,0},{4,2},{6,4},{0,6},{3,1},{5,3},{7,5},{1,7},{10,8},{12,10},{14... | collective-permute-start | bytes 13736 | tf_op jit(solution)/shard_map/ppermute | solution.py:77
  56.8 1.2 %collective-permute-start.12 = (f32[286,2,128]{2,0,1:T(8,128)S(1)}, f32[286,2,128]{2,0,1:T(8,128)S(1)}, u32[]{:S(2)}, u32[]{:S(2)}) collective-permute-start(f32[286,2,128]{2,0,1:T(8,128)S(1)} %fusion.15), channel_id=1, source_target_pairs={{1,0},{8,1},{9,8},{16,9},{17,16},{24,17},{25,24},{0,25},{3,2},{10,... | collective-permute-start | bytes 878600 | tf_op jit(solution)/shard_map/ppermute | solution.py:77
  58.0 1.1 %collective-permute-start.13 = (f32[286,2,2]{2,0,1:T(8,128)S(1)}, f32[286,2,2]{2,0,1:T(8,128)S(1)}, u32[]{:S(2)}, u32[]{:S(2)}) collective-permute-start(f32[286,2,2]{2,0,1:T(8,128)S(1)} %get-tuple-element.31), channel_id=1, source_target_pairs={{0,2},{2,4},{4,6},{6,0},{1,3},{3,5},{5,7},{7,1},{8,10},{10,12},{12... | collective-permute-start | bytes 13736 | tf_op jit(solution)/shard_map/ppermute | solution.py:77
  59.0 4.5 %collective-permute-done.14 = f32[286,2,2]{2,0,1:T(8,128)S(1)} collective-permute-done((f32[286,2,2]{2,0,1:T(8,128)S(1)}, f32[286,2,2]{2,0,1:T(8,128)S(1)}, u32[]{:S(2)}, u32[]{:S(2)}) %collective-permute-start.14) | collective-permute-done | bytes 4608 | tf_op jit(solution)/shard_map/ppermute | solution.py:77
  63.5 0.7 slice_bitcast_fusion.2
  64.2 3.9 %collective-permute-done.13 = f32[286,2,2]{2,0,1:T(8,128)S(1)} collective-permute-done((f32[286,2,2]{2,0,1:T(8,128)S(1)}, f32[286,2,2]{2,0,1:T(8,128)S(1)}, u32[]{:S(2)}, u32[]{:S(2)}) %collective-permute-start.13) | collective-permute-done | bytes 4608 | tf_op jit(solution)/shard_map/ppermute | solution.py:77
  68.1 0.7 slice_bitcast_fusion.4
  68.9 0.7 slice_bitcast_fusion.6
  69.6 0.7 slice_bitcast_fusion.10
  70.4 1.6 %concatenate.54 = f32[286,776]{1,0:T(8,128)S(1)} concatenate(f32[286,128]{1,0:T(8,128)} %get-tuple-element.39, f32[286,128]{1,0:T(8,128)} %get-tuple-element.38, f32[286,128]{1,0:T(8,128)} %get-tuple-element.37, f32[286,128]{1,0:T(8,128)} %get-tuple-element.36, f32[286,128]{1,0:T(8,128)} %get-tuple-element.35, f32[286,128]{1,0:T(8,128)} %get-tuple-element.34, ...), dimensions={1} | concatenate | bytes 1775488 | tf_op jit(solution)/shard_map/concatenate | solution.py:109
  72.0 2.7 %fusion.67 = f32[512,776]{0,1:T(8,128)S(1)} fusion(f32[286,512]{1,0:T(8,128)S(1)} %convolution_reduce_fusion, f32[286,776]{1,0:T(8,128)S(1)} %concatenate.54), kind=kOutput, calls=%fused_computation.128 | convolution fusion | flops 1363574784 | bytes 3062720 | tf_op jit(solution)/shard_map/dot_general | solution.py:107
  76.9 0.9 %copy.65 = f32[286,2,128]{2,1,0:T(2,128)} copy(f32[286,2,128]{2,0,1:T(8,128)S(1)} %fusion.12) | data formatting | bytes 585728 | tf_op jit(solution)/shard_map/add | solution.py:131
  (68 shorter events, 9.9 us)
Async XLA Ops:
  1.0 10.4 %copy-start.4 = (s32[512,10]{0,1:T(8,128)S(1)}, s32[512,10]{0,1:T(8,128)}, u32[]{:S(2)}) copy-start(s32[512,10]{0,1:T(8,128)} %param.10) | copy-start | bytes 61444
  1.0 10.5 %copy-start.6 = (f32[4]{0:T(128)S(1)}, f32[4]{0:T(128)}, u32[]{:S(2)}) copy-start(f32[4]{0:T(128)} %constant.91.clone) | copy-start | bytes 52
  1.0 11.9 %copy-start.5 = (f32[4,4,1]{1,0,2:T(4,128)S(1)}, f32[4,4,1]{1,0,2:T(4,128)}, u32[]{:S(2)}) copy-start(f32[4,4,1]{1,0,2:T(4,128)} %constant.105) | copy-start | bytes 196
  2.0 11.1 %copy-start.7 = (s32[286,10]{0,1:T(8,128)S(1)}, s32[286,10]{0,1:T(8,128)}, u32[]{:S(2)}) copy-start(s32[286,10]{0,1:T(8,128)} %param.11) | copy-start | bytes 34324
  2.1 41.1 %collective-permute-start.6 = (f32[286,2,128]{2,0,1:T(8,128)S(1)}, f32[286,2,128]{2,0,1:T(8,128)}, u32[]{:S(2)}, u32[]{:S(2)}) collective-permute-start(f32[286,2,128]{2,0,1:T(8,128)S(1)} %copy.54), channel_id=1, source_target_pairs={{1,0},{8,1},{9,8},{16,9},{17,16},{24,17},{25,24},{0,25},{3,2},{10,... | collective-permute-start | bytes 878600 | tf_op jit(solution)/shard_map/ppermute | solution.py:77
  6.6 38.3 %collective-permute-start.5 = (f32[286,2,128]{2,0,1:T(8,128)S(1)}, f32[286,2,128]{2,0,1:T(8,128)}, u32[]{:S(2)}, u32[]{:S(2)}) collective-permute-start(f32[286,2,128]{2,0,1:T(8,128)S(1)} %copy.54), channel_id=1, source_target_pairs={{0,1},{1,8},{8,9},{9,16},{16,17},{17,24},{24,25},{25,0},{2,3},{3,1... | collective-permute-start | bytes 878600 | tf_op jit(solution)/shard_map/ppermute | solution.py:77
  6.7 31.2 %collective-permute-start.2 = (f32[1,128,1,2,128]{4,3,0,1,2:T(2,128)S(1)}, f32[1,128,1,2,128]{4,3,0,1,2:T(2,128)S(1)}, u32[]{:S(2)}, u32[]{:S(2)}) collective-permute-start(f32[1,128,1,2,128]{4,3,0,1,2:T(2,128)S(1)} %get-tuple-element.25), channel_id=1, source_target_pairs={{0,24},{8,0},{16,8},{24,16},{1,25},{9,1},{17,9},{25,17},{2,26},{10... | collective-permute-start | bytes 393224 | tf_op jit(solution)/shard_map/ppermute | solution.py:41
  7.9 22.1 %collective-permute-start = (f32[1,128,1,2,128]{4,3,0,1,2:T(2,128)S(1)}, f32[1,128,1,2,128]{4,3,0,1,2:T(2,128)S(1)}, u32[]{:S(2)}, u32[]{:S(2)}) collective-permute-start(f32[1,128,1,2,128]{4,3,0,1,2:T(2,128)S(1)} %get-tuple-element.26), channel_id=1, source_target_pairs={{0,8},{8,16},{16,24},{24,0},{1,9},{9,17},{17,25},{25,1},{2,10},{10... | collective-permute-start | bytes 393224 | tf_op jit(solution)/shard_map/ppermute | solution.py:41
  9.0 9.3 %collective-permute-start.8 = (f32[286,2,2]{2,0,1:T(8,128)S(1)}, f32[286,2,2]{2,0,1:T(8,128)S(1)}, u32[]{:S(2)}, u32[]{:S(2)}) collective-permute-start(f32[286,2,2]{2,0,1:T(8,128)S(1)} %get-tuple-element.42), channel_id=1, source_target_pairs={{2,0},{4,2},{6,4},{0,6},{3,1},{5,3},{7,5},{1,7},{10,8},{12,10},{14... | collective-permute-start | bytes 13736 | tf_op jit(solution)/shard_map/ppermute | solution.py:77
  18.3 11.0 %collective-permute-start.7 = (f32[286,2,2]{2,0,1:T(8,128)S(1)}, f32[286,2,2]{2,0,1:T(8,128)S(1)}, u32[]{:S(2)}, u32[]{:S(2)}) collective-permute-start(f32[286,2,2]{2,0,1:T(8,128)S(1)} %get-tuple-element.43), channel_id=1, source_target_pairs={{0,2},{2,4},{4,6},{6,0},{1,3},{3,5},{5,7},{7,1},{8,10},{10,12},{12... | collective-permute-start | bytes 13736 | tf_op jit(solution)/shard_map/ppermute | solution.py:77
  29.2 8.6 %collective-permute-start.1 = (f32[1,128,1,2,128]{4,3,0,1,2:T(2,128)S(1)}, f32[1,128,1,2,128]{4,3,0,1,2:T(2,128)S(1)}, u32[]{:S(2)}, u32[]{:S(2)}) collective-permute-start(f32[1,128,1,2,128]{4,3,0,1,2:T(2,128)S(1)} %get-tuple-element.27), channel_id=1, source_target_pairs={{0,16},{8,24},{16,0},{24,8},{1,17},{9,25},{17,1},{25,9},{2,18},{10... | collective-permute-start | bytes 393224 | tf_op jit(solution)/shard_map/ppermute | solution.py:41
  38.5 4.6 %collective-permute-start.3 = (f32[512,2,1]{0,2,1:T(1,128)S(1)}, f32[512,2,1]{0,2,1:T(1,128)S(1)}, u32[]{:S(2)}, u32[]{:S(2)}) collective-permute-start(f32[512,2,1]{0,2,1:T(1,128)S(1)} %get-tuple-element.23), channel_id=1, source_target_pairs={{0,2},{2,4},{4,6},{6,0},{1,3},{3,5},{5,7},{7,1},{8,10},{10,12},{12... | collective-permute-start | bytes 12296 | tf_op jit(solution)/shard_map/ppermute | solution.py:77
  39.5 3.7 %collective-permute-start.4 = (f32[512,2,1]{0,2,1:T(1,128)S(1)}, f32[512,2,1]{0,2,1:T(1,128)S(1)}, u32[]{:S(2)}, u32[]{:S(2)}) collective-permute-start(f32[512,2,1]{0,2,1:T(1,128)S(1)} %get-tuple-element.24), channel_id=1, source_target_pairs={{2,0},{4,2},{6,4},{0,6},{3,1},{5,3},{7,5},{1,7},{10,8},{12,10},{14... | collective-permute-start | bytes 12296 | tf_op jit(solution)/shard_map/ppermute | solution.py:77
  41.6 9.5 %collective-permute-start.10 = (f32[512,128]{0,1:T(8,128)S(1)}, f32[512,128]{0,1:T(8,128)S(1)}, u32[]{:S(2)}, u32[]{:S(2)}) collective-permute-start(f32[512,128]{0,1:T(8,128)S(1)} %get-tuple-element.21), channel_id=1, source_target_pairs={{1,0},{8,1},{9,8},{16,9},{17,16},{24,17},{25,24},{0,25},{3,2},{10,... | collective-permute-start | bytes 786440 | tf_op jit(solution)/shard_map/ppermute | solution.py:77
  43.1 8.0 %collective-permute-start.9 = (f32[512,128]{0,1:T(8,128)S(1)}, f32[512,128]{0,1:T(8,128)S(1)}, u32[]{:S(2)}, u32[]{:S(2)}) collective-permute-start(f32[512,128]{0,1:T(8,128)S(1)} %get-tuple-element.22), channel_id=1, source_target_pairs={{0,1},{1,8},{8,9},{9,16},{16,17},{17,24},{24,25},{25,0},{2,3},{3,1... | collective-permute-start | bytes 786440 | tf_op jit(solution)/shard_map/ppermute | solution.py:77
  51.1 0.7 copy-start.2
  51.8 1.0 %copy-start = (f32[286,2,128]{2,1,0:T(2,128)S(1)}, f32[286,2,128]{2,1,0:T(2,128)}, u32[]{:S(2)}) copy-start(f32[286,2,128]{2,1,0:T(2,128)} %param.7) | copy-start | bytes 878596
  51.8 1.0 %copy-start.1 = (f32[286,2,128]{2,1,0:T(2,128)S(1)}, f32[286,2,128]{2,1,0:T(2,128)}, u32[]{:S(2)}) copy-start(f32[286,2,128]{2,1,0:T(2,128)} %param.8) | copy-start | bytes 878596
  53.1 10.4 %collective-permute-start.14 = (f32[286,2,2]{2,0,1:T(8,128)S(1)}, f32[286,2,2]{2,0,1:T(8,128)S(1)}, u32[]{:S(2)}, u32[]{:S(2)}) collective-permute-start(f32[286,2,2]{2,0,1:T(8,128)S(1)} %get-tuple-element.30), channel_id=1, source_target_pairs={{2,0},{4,2},{6,4},{0,6},{3,1},{5,3},{7,5},{1,7},{10,8},{12,10},{14... | collective-permute-start | bytes 13736 | tf_op jit(solution)/shard_map/ppermute | solution.py:77
  56.8 12.1 %collective-permute-start.12 = (f32[286,2,128]{2,0,1:T(8,128)S(1)}, f32[286,2,128]{2,0,1:T(8,128)S(1)}, u32[]{:S(2)}, u32[]{:S(2)}) collective-permute-start(f32[286,2,128]{2,0,1:T(8,128)S(1)} %fusion.15), channel_id=1, source_target_pairs={{1,0},{8,1},{9,8},{16,9},{17,16},{24,17},{25,24},{0,25},{3,2},{10,... | collective-permute-start | bytes 878600 | tf_op jit(solution)/shard_map/ppermute | solution.py:77
  58.0 11.6 %collective-permute-start.11 = (f32[286,2,128]{2,0,1:T(8,128)S(1)}, f32[286,2,128]{2,0,1:T(8,128)S(1)}, u32[]{:S(2)}, u32[]{:S(2)}) collective-permute-start(f32[286,2,128]{2,0,1:T(8,128)S(1)} %fusion.15), channel_id=1, source_target_pairs={{0,1},{1,8},{8,9},{9,16},{16,17},{17,24},{24,25},{25,0},{2,3},{3,1... | collective-permute-start | bytes 878600 | tf_op jit(solution)/shard_map/ppermute | solution.py:77
  58.0 10.1 %collective-permute-start.13 = (f32[286,2,2]{2,0,1:T(8,128)S(1)}, f32[286,2,2]{2,0,1:T(8,128)S(1)}, u32[]{:S(2)}, u32[]{:S(2)}) collective-permute-start(f32[286,2,2]{2,0,1:T(8,128)S(1)} %get-tuple-element.31), channel_id=1, source_target_pairs={{0,2},{2,4},{4,6},{6,0},{1,3},{3,5},{5,7},{7,1},{8,10},{10,12},{12... | collective-permute-start | bytes 13736 | tf_op jit(solution)/shard_map/ppermute | solution.py:77
  74.7 1.0 %copy-start.3 = (f32[512,128]{0,1:T(8,128)S(1)}, f32[512,128]{0,1:T(8,128)}, u32[]{:S(2)}) copy-start(f32[512,128]{0,1:T(8,128)} %copy-done.2) | copy-start | bytes 786436
